TPU v7x, 32 devices: a whole 2x2x4 slice. The times are simulated.
32 devices in a mesh: wide: 8 (over z, x), narrow: 4 (over y, core).
Axes of the slice: x: 2, y: 2, z: 4, core: 2. Of those that a mesh axis runs over, the one named last changes fastest.
Arguments:
- tokens: bfloat16 [16384, 2048], P(('wide', 'narrow')), may hold values from -6 to 6
- lengths: int32 [32], P(('wide', 'narrow')), may hold values from 1 to 512, 12288 in all
- in_weight: bfloat16 [2048, 8512], P(('wide', 'narrow')), may hold values from -0.125 to 0.125
- out_weight: bfloat16 [4096, 2048], P(('wide', 'narrow')), may hold values from -0.09375 to 0.09375
- norm_gain: bfloat16 [2048], P(('wide', 'narrow')), may hold values from 0.5 to 1.5
- conv_weight: bfloat16 [4352, 4], P(('wide', 'narrow')), may hold values from -3 to 3
- conv_bias: bfloat16 [4352], P(('wide', 'narrow')), may hold values from -0.5 to 0.5
- out_gain: bfloat16 [4096], P(('wide', 'narrow')), may hold values from 0.5 to 1.5
- a_log: float32 [64], P('wide'), may hold values from -3 to 1.6
- dt_bias: float32 [64], P('wide'), may hold values from -6 to -3
- d_skip: float32 [64], P('wide'), may hold values from 0.5 to 1.5
- cotangent: bfloat16 [16384, 2048], P(('wide', 'narrow')), may hold values from -6 to 6
Outputs:
- output: bfloat16 [16384, 2048], P(('wide', 'narrow'))
- token_grad: bfloat16 [16384, 2048], P(('wide', 'narrow'))
- in_weight_grad: float32 [2048, 8512], P(('wide', 'narrow'))
- out_weight_grad: float32 [4096, 2048], P(('wide', 'narrow'))
- norm_gain_grad: float32 [2048], P(('wide', 'narrow'))
- conv_weight_grad: float32 [4352, 4], P(('wide', 'narrow'))
- conv_bias_grad: float32 [4352], P(('wide', 'narrow'))
- out_gain_grad: float32 [4096], P(('wide', 'narrow'))
- a_log_grad: float32 [64], P('wide')
- dt_bias_grad: float32 [64], P('wide')
- d_skip_grad: float32 [64], P('wide')
Inputs may be any that keep to these rules, and one draw needn't show every extreme that they name: `lengths`: each sequence's live tokens are the first rows of its 512 slots; the longest fills all of them.
All inputs are finite; a program needn't handle non-finite values. No bound on the sum of `lengths` on one device may be relied on, other than what follows from the above.
Results may differ from a plain program's by a relative error of at most 0.014.
Values may be sent and summed in bfloat16 or wider, within the bound.
No kernel may reach another device: no remote copies, remote signals or barrier semaphores. Data moves between devices by JAX's collectives and lax.ppermute only.
A program may use at most 448 MiB of HBM per device.

v0:
```python
from functools import partial
import jax
import jax.numpy as jnp
from jax import lax
from jax.sharding import PartitionSpec as P

HEADS = 64
HEAD_DIM = 64
NSTATE = 128
KCONV = 4
SPAN = 256
EPS = 1e-05


def rounded(values):
    fixed = lax.stop_gradient(values)
    coarse = lax.optimization_barrier(fixed.astype(jnp.bfloat16)).astype(jnp.float32)
    return values + (coarse - fixed)


def rms_scale(values, gain_vec):
    return values * lax.rsqrt(jnp.mean(values * values, axis=-1, keepdims=True) + EPS) * gain_vec


def block_step(carry_state, pieces, rounding):
    x_rows, b_rows, c_rows, dt_rows, log_decay = pieces
    block_len = x_rows.shape[0]
    head_count = dt_rows.shape[1]
    cum_decay = jnp.cumsum(log_decay, axis=0).T
    c_dot_b = jnp.dot(c_rows, b_rows.T, preferred_element_type=jnp.float32)
    lower_mask = (
        lax.iota(jnp.int32, block_len)[:, None] >= lax.iota(jnp.int32, block_len)[None, :]
    )[None]
    spread_log = cum_decay[:, :, None] - cum_decay[:, None, :]
    decays = jnp.where(lower_mask, jnp.exp(jnp.where(lower_mask, spread_log, 0.0)), 0.0)
    mixing = rounding(c_dot_b[None] * decays * dt_rows.T[:, None, :])
    x_heads = x_rows.reshape(block_len, head_count, -1)
    within = jnp.einsum("hts,shp->thp", mixing, x_heads, preferred_element_type=jnp.float32)
    carried = (
        jnp.einsum("tn,hnp->thp", c_rows, carry_state, preferred_element_type=jnp.float32)
        * jnp.exp(cum_decay).T[:, :, None]
    )
    end_decay = cum_decay[:, -1:]
    entry_scale = jnp.exp(end_decay - cum_decay) * dt_rows.T
    fresh_state = jnp.einsum(
        "sn,hs,shp->hnp", b_rows, entry_scale, x_heads, preferred_element_type=jnp.float32
    )
    carry_state = carry_state * jnp.exp(end_decay)[:, :, None] + fresh_state
    return (carry_state, (within + carried).reshape(block_len, -1))


def ssd_mixer(projected, conv_w, conv_b, log_rate, rate_bias, skip_gain, gain_out, rounding):
    seq_len = projected.shape[0]
    inner_width = HEADS * HEAD_DIM
    channels = inner_width + 2 * NSTATE
    gate_part = projected[:, :inner_width]
    conv_in = projected[:, inner_width : inner_width + channels]
    dt_raw = projected[:, inner_width + channels :]
    padded = jnp.pad(conv_in, ((KCONV - 1, 0), (0, 0)))
    conv_out = conv_b
    for tap_idx in range(KCONV):
        conv_out = conv_out + padded[tap_idx : tap_idx + seq_len] * conv_w[:, tap_idx]
    active = jax.nn.silu(conv_out)
    x_rows = rounding(active[:, :inner_width])
    b_rows = rounding(active[:, inner_width : inner_width + NSTATE])
    c_rows = rounding(active[:, inner_width + NSTATE :])
    dt_rows = jax.nn.softplus(dt_raw + rate_bias)
    log_decay = -dt_rows * jnp.exp(log_rate)
    block_count = seq_len // SPAN

    def to_blocks(values):
        return values.reshape(block_count, SPAN, values.shape[1])

    zero_state = jnp.zeros((HEADS, NSTATE, HEAD_DIM), jnp.float32)
    _, block_outs = lax.scan(
        jax.checkpoint(partial(block_step, rounding=rounding)),
        zero_state,
        (
            to_blocks(x_rows),
            to_blocks(b_rows),
            to_blocks(c_rows),
            to_blocks(dt_rows),
            to_blocks(log_decay),
        ),
    )
    ssd_out = block_outs.reshape(seq_len, inner_width) + x_rows * jnp.repeat(skip_gain, HEAD_DIM)
    gated_out = ssd_out * jax.nn.silu(gate_part)
    return rms_scale(gated_out, gain_out)


def fetch_weights(in_part, out_part, norm_part, conv_part, bias_part, gain_part):
    return (
        lax.all_gather(in_part, ("wide", "narrow"), axis=0, tiled=True),
        lax.all_gather(out_part, ("wide", "narrow"), axis=0, tiled=True),
        lax.all_gather(norm_part, ("wide", "narrow"), axis=0, tiled=True),
        lax.all_gather(conv_part, ("wide", "narrow"), axis=0, tiled=True),
        lax.all_gather(bias_part, ("wide", "narrow"), axis=0, tiled=True),
        lax.all_gather(gain_part, ("wide", "narrow"), axis=0, tiled=True),
    )


def spread_heads(head_grad, wide_count, narrow_count):
    share_len = head_grad.shape[0] // wide_count
    blocks = jnp.broadcast_to(
        head_grad.reshape(wide_count, 1, share_len), (wide_count, narrow_count, share_len)
    )
    return blocks.reshape(-1)


def settle_grads(
    normed_low,
    proj_grad,
    mixed_low,
    branch_grad,
    norm_term,
    conv_term,
    bias_term,
    gain_term,
    head_terms,
):
    wide_count = lax.axis_size("wide")
    narrow_count = lax.axis_size("narrow")
    heads_laid = [spread_heads(head_term, wide_count, narrow_count) for head_term in head_terms]
    columns = normed_low
    inw_own = lax.psum_scatter(
        lax.dot_general(
            columns, proj_grad, (((0,), (0,)), ((), ())), preferred_element_type=jnp.float32
        ).astype(jnp.bfloat16),
        ("wide", "narrow"),
        scatter_dimension=0,
        tiled=True,
    ).astype(jnp.float32)
    columns = mixed_low
    outw_own = lax.psum_scatter(
        lax.dot_general(
            columns, branch_grad, (((0,), (0,)), ((), ())), preferred_element_type=jnp.float32
        ).astype(jnp.bfloat16),
        ("wide", "narrow"),
        scatter_dimension=0,
        tiled=True,
    ).astype(jnp.float32)
    small_own = (
        lax.psum_scatter(norm_term, ("wide", "narrow"), scatter_dimension=0, tiled=True),
        lax.psum_scatter(conv_term, ("wide", "narrow"), scatter_dimension=0, tiled=True),
        lax.psum_scatter(bias_term, ("wide", "narrow"), scatter_dimension=0, tiled=True),
        lax.psum_scatter(gain_term, ("wide", "narrow"), scatter_dimension=0, tiled=True),
        lax.psum_scatter(heads_laid[0], ("wide", "narrow"), scatter_dimension=0, tiled=True),
        lax.psum_scatter(heads_laid[1], ("wide", "narrow"), scatter_dimension=0, tiled=True),
        lax.psum_scatter(heads_laid[2], ("wide", "narrow"), scatter_dimension=0, tiled=True),
    )
    return (inw_own, outw_own) + tuple(small_own)


def body(
    tokens,
    lengths,
    in_weight,
    out_weight,
    norm_gain,
    conv_weight,
    conv_bias,
    out_gain,
    a_log,
    dt_bias,
    d_skip,
    cotangent,
):
    row_count = tokens.shape[0]
    live_mask = (lax.iota(jnp.int32, row_count) < lengths[0]).astype(jnp.float32)[:, None]
    gathered = fetch_weights(in_weight, out_weight, norm_gain, conv_weight, conv_bias, out_gain)
    head_values = (
        lax.all_gather(a_log, "wide", axis=0, tiled=True),
        lax.all_gather(dt_bias, "wide", axis=0, tiled=True),
        lax.all_gather(d_skip, "wide", axis=0, tiled=True),
    )
    source = tokens.astype(jnp.float32)
    normed, front_back = jax.vjp(rms_scale, source, gathered[2].astype(jnp.float32))
    normed_low = normed.astype(jnp.bfloat16)
    projected = jnp.dot(normed_low, gathered[0], preferred_element_type=jnp.float32)

    def mix_local(proj_rows, conv_w, conv_b, log_rate, rate_bias, skip_gain, gain_out):
        return ssd_mixer(
            proj_rows, conv_w, conv_b, log_rate, rate_bias, skip_gain, gain_out, rounded
        )

    mixed, mix_back = jax.vjp(
        mix_local,
        projected,
        gathered[3].astype(jnp.float32),
        gathered[4].astype(jnp.float32),
        head_values[0],
        head_values[1],
        head_values[2],
        gathered[5].astype(jnp.float32),
    )
    mixed_low = mixed.astype(jnp.bfloat16)
    branch = jnp.dot(mixed_low, gathered[1], preferred_element_type=jnp.float32)
    output = (source + live_mask * branch).astype(jnp.bfloat16)
    gathered = fetch_weights(in_weight, out_weight, norm_gain, conv_weight, conv_bias, out_gain)
    cot_rows = cotangent.astype(jnp.float32)
    branch_grad = (live_mask * cot_rows).astype(jnp.bfloat16)
    mixed_grad = lax.dot_general(
        branch_grad, gathered[1], (((1,), (1,)), ((), ())), preferred_element_type=jnp.float32
    )
    mix_grads = mix_back(mixed_grad)
    proj_grad = mix_grads[0].astype(jnp.bfloat16)
    normed_grad = lax.dot_general(
        proj_grad, gathered[0], (((1,), (1,)), ((), ())), preferred_element_type=jnp.float32
    )
    source_grad, normgain_grad = front_back(normed_grad)
    token_grad = (cot_rows + source_grad).astype(jnp.bfloat16)
    owned = settle_grads(
        normed_low,
        proj_grad,
        mixed_low,
        branch_grad,
        normgain_grad,
        mix_grads[1],
        mix_grads[2],
        mix_grads[6],
        (mix_grads[3], mix_grads[4], mix_grads[5]),
    )
    return (
        output,
        token_grad,
        owned[0],
        owned[1],
        owned[2],
        owned[3],
        owned[4],
        owned[5],
        owned[6],
        owned[7],
        owned[8],
    )


def solution(mesh):
    in_specs = (
        P(("wide", "narrow"), None),
        P(("wide", "narrow")),
        P(("wide", "narrow"), None),
        P(("wide", "narrow"), None),
        P(("wide", "narrow")),
        P(("wide", "narrow"), None),
        P(("wide", "narrow")),
        P(("wide", "narrow")),
        P("wide"),
        P("wide"),
        P("wide"),
        P(("wide", "narrow"), None),
    )
    out_specs = (
        P(("wide", "narrow"), None),
        P(("wide", "narrow"), None),
        P(("wide", "narrow"), None),
        P(("wide", "narrow"), None),
        P(("wide", "narrow")),
        P(("wide", "narrow"), None),
        P(("wide", "narrow")),
        P(("wide", "narrow")),
        P("wide"),
        P("wide"),
        P("wide"),
    )
    return jax.shard_map(body, mesh=mesh, in_specs=in_specs, out_specs=out_specs, check_vma=False)
```

profile of v0, /device:TPU:1, one launch (start us, length us, event | category | flops | bytes accessed | tf_op | source)
XLA Modules:
  0.0 1708.1 jit_solution(17202813251286906501)
XLA Ops:
  13.8 19.4 %all-reduce.29 = (f32[64]{0:T(128)S(1)}, f32[64]{0:T(128)S(1)}, f32[64]{0:T(128)S(1)}) all-reduce(f32[64]{0:T(128)S(1)} %dynamic-update-slice.1, f32[64]{0:T(128)S(1)} %dynamic-update-slice.2, f32[64]{0:T(128)S(1)} %dynamic-update-slice.4), channel_id=1, replica_groups=mesh['wide'=8,'narrow'=4] {'wide'}, use_global_device_ids=true, to_apply=%add.17 | all-reduce | flops 192 | bytes 1536
  35.4 45.5 %all-reduce.30 = (bf16[2048]{0:T(1024)(128)(2,1)S(1)}, bf16[4352]{0:T(1024)(128)(2,1)S(1)}) all-reduce(bf16[2048]{0:T(1024)(128)(2,1)S(1)} %dynamic-update-slice, bf16[4352]{0:T(1024)(128)(2,1)S(1)} %dynamic-update-slice.3), channel_id=1, replica_groups=mesh['wide'=8,'narrow'=4] {'wide','narrow'}, use_global_device_ids=true, to_apply=%add.16 | all-reduce | flops 6400 | bytes 25600
  81.0 42.1 %all-gather.1 = bf16[32,1,128]{2,1,0:T(2,128)(2,1)S(1)} all-gather(bf16[1,1,128]{2,1,0:T(2,128)(2,1)} %bitcast.427), channel_id=1, replica_groups=mesh['wide'=8,'narrow'=4] {'wide','narrow'}, dimensions={0}, use_global_device_ids=true | all-gather | bytes 8448 | tf_op jit(solution)/shard_map/all_gather | solution.py:98
  124.5 39.0 %all-gather = bf16[32,136,4]{1,2,0:T(4,128)(2,1)S(1)} all-gather(bf16[1,136,4]{1,2,0:T(4,128)(2,1)} %bitcast.426), channel_id=1, replica_groups=mesh['wide'=8,'narrow'=4] {'wide','narrow'}, dimensions={0}, use_global_device_ids=true | all-gather | bytes 35904 | tf_op jit(solution)/shard_map/all_gather | solution.py:96
  166.6 50.0 %all-gather.5.cloned.1.call-done = bf16[2048,8512]{1,0:T(8,128)(2,1)} async-done(((bf16[64,8512]{1,0:T(8,128)(2,1)}), bf16[2048,8512]{1,0:T(8,128)(2,1)}) %all-gather.5.cloned.1.call-update) | async-done | bytes 34865168 | tf_op jit(solution)/shard_map/all_gather | solution.py:93
  216.6 26.2 %fusion.100 = f32[512,8512]{0,1:T(8,128)} fusion(bf16[2048,8512]{1,0:T(8,128)(2,1)} %all-gather.5.cloned.1.call-done, bf16[512,2048]{1,0:T(8,128)(2,1)} %param.16, f32[2048]{0:T(1024)S(1)} %convert_element_type.107, f32[512]{0:T(512)S(1)} %fusion.106), kind=kOutput, calls=%fused_computation.183 | convolution fusion | flops 17855152128 | bytes 54405120 | tf_op jit(solution)/shard_map/dot_general | solution.py:179
  253.5 23.8 %fusion.81 = (f32[512,4352]{0,1:T(8,128)S(1)}, f32[512,4352]{0,1:T(8,128)}) fusion(f32[512,4352]{0,1:T(8,128)} %slice.132, f32[4352]{0:T(1024)S(1)} %get-tuple-element.725, f32[4352]{0:T(1024)S(1)} %get-tuple-element.726, f32[4352]{0:T(1024)S(1)} %get-tuple-element.727, f32[4352]{0:T(1024)S(1)} %get-tuple-element.724, f32[4352]{0:T(1024)S(1)} %convert_element_type.109), kind=kLoop, calls=%fused_computation.144 | loop fusion | flops 26738688 | bytes 26825728 | tf_op jit(solution)/shard_map/jvp(jit(silu))/mul | solution.py:63
  302.9 257.0 %while.44 = (s32[]{:T(128)}, f32[64,128,64]{1,2,0:T(8,128)S(1)}, f32[2,256,4096]{1,0,2:T(2,128)}, f32[2,64,128,64]{2,3,1,0:T(8,128)}, f32[2,256,64]{1,2,0:T(8,12...) while((s32[]{:T(128)}, f32[64,128,64]{1,2,0:T(8,128)S(1)}, ...), condition=%wide.region_4.5_spmd.clone.clone, body=%wide.region_1.4_spmd.clone.clone.sunk | while | flops 1156104448 | bytes 122035080 | solution.py:75
  329.0 19.2 %copy.361 = f32[1,256,4096]{1,0,2:T(1,128)} copy(f32[1,256,4096]{1,2,0:T(8,128)S(1)} %bitcast.404) | data formatting | bytes 8388608 | tf_op jit(solution)/shard_map/jvp()/while/body/jit(dynamic_update_index_in_dim)/dynamic_update_slice | solution.py:75
  348.2 83.3 %dynamic_update_slice.87 = f32[2,256,4096]{1,0,2:T(2,128)} dynamic-update-slice(f32[2,256,4096]{1,0,2:T(2,128)} %get-tuple-element.1047, f32[1,256,4096]{1,0,2:T(1,128)} %copy.361, s32[]{:T(128)S(6)} %copy.378, s32[]{:T(128)} %constant.121.clone.1..sunk.1, s32[]{:T(128)} %constant.121.clone.1..sunk.1) | dynamic-update-slice | bytes 8388612 | tf_op jit(solution)/shard_map/jvp()/while/body/jit(dynamic_update_index_in_dim)/dynamic_update_slice | solution.py:75
  457.3 19.2 %copy.361 = f32[1,256,4096]{1,0,2:T(1,128)} copy(f32[1,256,4096]{1,2,0:T(8,128)S(1)} %bitcast.404) | data formatting | bytes 8388608 | tf_op jit(solution)/shard_map/jvp()/while/body/jit(dynamic_update_index_in_dim)/dynamic_update_slice | solution.py:75
  476.4 83.3 %dynamic_update_slice.87 = f32[2,256,4096]{1,0,2:T(2,128)} dynamic-update-slice(f32[2,256,4096]{1,0,2:T(2,128)} %get-tuple-element.1047, f32[1,256,4096]{1,0,2:T(1,128)} %copy.361, s32[]{:T(128)S(6)} %copy.378, s32[]{:T(128)} %constant.121.clone.1..sunk.1, s32[]{:T(128)} %constant.121.clone.1..sunk.1) | dynamic-update-slice | bytes 8388612 | tf_op jit(solution)/shard_map/jvp()/while/body/jit(dynamic_update_index_in_dim)/dynamic_update_slice | solution.py:75
  575.1 17.8 %multiply_reduce_fusion.10 = (f32[4096]{0:T(1024)}, f32[512]{0:T(512)S(1)}, f32[512,4096]{0,1:T(8,128)}) fusion(f32[512,4096]{0,1:T(8,128)} %get-tuple-element.795, f32[512]{0:T(512)S(1)} %fusion.107, f32[4096]{0:T(1024)S(1)} %bitcast.422, bf16[4096,2048]{1,0:T(8,128)(2,1)} %all-gather.7.cloned.1.call-done, bf16[512,2048]{1,0:T(8,128)(2,1)S(1)} %copy-done.19, ...), kind=kOutput, calls=%fused_computation.150 | convolution fusion | flops 8605659136 | bytes 35690496 | tf_op jit(solution)/shard_map/dot_general | solution.py:202
  592.9 18.1 %multiply_reduce_fusion.9 = (f32[4096]{0:T(1024)}, f32[512,4096]{0,1:T(8,128)}, f32[512,4096]{0,1:T(8,128)}) fusion(f32[512,4096]{0,1:T(8,128)} %copy-done.2, f32[512,8512]{0,1:T(8,128)} %fusion.100, f32[512,4096]{0,1:T(8,128)} %get-tuple-element.795, f32[512]{0:T(512)S(1)} %multiply_multiply_fusion.4, f32[512]{0:T(512)S(1)} %fusion.107, ...), kind=kLoop, calls=%fused_computation.149 | loop fusion | flops 44036096 | bytes 58773504 | tf_op jit(solution)/shard_map/transpose(jvp())/reduce_sum | solution.py:86
  629.8 342.9 %while.43 = (s32[]{:T(128)}, f32[64,128,64]{1,2,0:T(8,128)}, f32[2,256,4096]{1,0,2:T(2,128)}, f32[2,256,128]{2,1,0:T(8,128)}, f32[2,256,128]{2,1,0:T(8,128)}, /*...) while((s32[]{:T(128)}, f32[64,128,64]{1,2,0:T(8,128)}, ...), condition=%wide.region_19.20_spmd.clone, body=%wide.region_7.19_spmd.clone.sunk | while | flops 2587640576 | bytes 238366704 | solution.py:75
  657.0 16.5 fusion.205
  677.6 11.4 bitcast_add_fusion.12
  693.3 19.1 %copy.353 = f32[1,256,4096]{1,0,2:T(1,128)} copy(f32[1,256,4096]{1,2,0:T(8,128)S(1)} %bitcast.402) | data formatting | bytes 8388608 | tf_op jit(solution)/shard_map/transpose(jvp())/while/body/jit(dynamic_update_index_in_dim)/dynamic_update_slice | solution.py:75
  716.9 83.3 %dynamic_update_slice.84 = f32[2,256,4096]{1,0,2:T(2,128)} dynamic-update-slice(f32[2,256,4096]{1,0,2:T(2,128)} %get-tuple-element.1090, f32[1,256,4096]{1,0,2:T(1,128)} %copy.353, s32[]{:T(128)S(6)} %sub.332, s32[]{:T(128)} %constant.121.clone.1..sunk, s32[]{:T(128)} %constant.121.clone.1..sunk) | dynamic-update-slice | bytes 8388612 | tf_op jit(solution)/shard_map/transpose(jvp())/while/body/jit(dynamic_update_index_in_dim)/dynamic_update_slice | solution.py:75
  829.4 16.5 fusion.205
  865.6 19.1 %copy.353 = f32[1,256,4096]{1,0,2:T(1,128)} copy(f32[1,256,4096]{1,2,0:T(8,128)S(1)} %bitcast.402) | data formatting | bytes 8388608 | tf_op jit(solution)/shard_map/transpose(jvp())/while/body/jit(dynamic_update_index_in_dim)/dynamic_update_slice | solution.py:75
  889.2 83.3 %dynamic_update_slice.84 = f32[2,256,4096]{1,0,2:T(2,128)} dynamic-update-slice(f32[2,256,4096]{1,0,2:T(2,128)} %get-tuple-element.1090, f32[1,256,4096]{1,0,2:T(1,128)} %copy.353, s32[]{:T(128)S(6)} %sub.332, s32[]{:T(128)} %constant.121.clone.1..sunk, s32[]{:T(128)} %constant.121.clone.1..sunk) | dynamic-update-slice | bytes 8388612 | tf_op jit(solution)/shard_map/transpose(jvp())/while/body/jit(dynamic_update_index_in_dim)/dynamic_update_slice | solution.py:75
  985.3 27.8 %multiply_reduce_fusion.7 = (f32[4352]{0:T(1024)S(1)}, f32[4352]{0:T(1024)S(1)}, f32[4352]{0:T(1024)S(1)}, f32[4352]{0:T(1024)S(1)}, f32[4352]{0:T(1024)S(1)}, /*index=5*/f32[512,4352]{0,1:T(8,128)}) fusion(f32[512,4352]{0,1:T(8,128)} %slice.132, f32[512,8512]{0,1:T(8,128)} %fusion.100, f32[512,4352]{0,1:T(8,128)} %get-tuple-element.797, ...), kind=kLoop, calls=%fused_computation.141 | loop fusion | flops 44542720 | bytes 44651520 | tf_op jit(solution)/shard_map/transpose(jvp())/reduce_sum | solution.py:62
  1014.0 16.3 convolution_convert_fusion.1
  1032.6 12.4 broadcast_multiply_fusion
  1045.0 14.4 pad_add_fusion
  1059.4 28.2 %convolution_convert_fusion = bf16[2048,8512]{1,0:T(8,128)(2,1)} fusion(bf16[512,2048]{1,0:T(8,128)(2,1)S(1)} %copy-done.13, f32[2048]{0:T(1024)S(1)} %copy-done.50, f32[512]{0:T(512)S(1)} %copy-done.57, f32[512,4096]{0,1:T(8,128)} %get-tuple-element.814, f32[512,4352]{0,1:T(8,128)} %pad_add_fusion, f32[512,64]{0,1:T(8,128)S(1)} %get-tuple-element.792), kind=kOutput, calls=%fused_computation.124 | convolution fusion | flops 17885659136 | bytes 54405120 | tf_op jit(solution)/shard_map/dot_general | solution.py:126
  1089.2 36.0 %fusion.88 = (f32[2048]{0:T(1024)S(1)}, f32[512]{0:T(512)S(1)}, f32[512,2048]{1,0:T(8,128)}) fusion(bf16[512,2048]{1,0:T(8,128)(2,1)S(1)} %copy-done.13, f32[512]{0:T(512)S(1)} %copy-done.57, f32[2048]{0:T(1024)S(1)} %copy-done.50, bf16[2048,8512]{1,0:T(8,128)(2,1)} %all-gather.5.cloned.1.call-done, f32[512,4096]{0,1:T(8,128)} %get-tuple-element.814, ...), kind=kOutput, calls=%fused_computation.174 | convolution fusion | flops 17871370240 | bytes 58609664 | tf_op jit(solution)/shard_map/dot_general | solution.py:207
  1125.2 43.6 %all-reduce.28 = (f32[2048]{0:T(1024)S(1)}, f32[4352]{0:T(1024)S(1)}, f32[4096]{0:T(1024)S(1)}, f32[256]{0:T(256)S(1)}, f32[256]{0:T(256)S(1)}, /*index=5*/f32[256]{0:T(256)S(1)}) all-reduce(f32[2048]{0:T(1024)S(1)} %get-tuple-element.722, ...), channel_id=4, replica_groups=mesh['wide'=8,'narrow'=4] {'wide','narrow'}, use_global_device_ids=true, to_apply=%region_24.25.clone | all-reduce | flops 11264 | bytes 90112
  1177.9 16.2 fusion.92
  1195.5 125.1 %reduce-scatter.6.cloned.1.call-done = bf16[128,2048]{1,0:T(8,128)(2,1)} async-done(((bf16[4096,2048]{1,0:T(8,128)(2,1)}), bf16[128,2048]{1,0:T(8,128)(2,1)}) %reduce-scatter.6.cloned.1.call-update) | async-done | bytes 524304 | tf_op jit(solution)/shard_map/reduce_scatter | solution.py:134
  1322.7 375.7 %reduce-scatter.4.cloned.1.call-done = bf16[64,8512]{1,0:T(8,128)(2,1)} async-done(((bf16[2048,8512]{1,0:T(8,128)(2,1)}), bf16[64,8512]{1,0:T(8,128)(2,1)}) %reduce-scatter.4.cloned.1.call-update) | async-done | bytes 1089552 | tf_op jit(solution)/shard_map/reduce_scatter | solution.py:125
  (413 shorter events, 257.8 us)
Async XLA Ops:
  7.2 209.5 %all-gather.5.cloned.1.call-start = ((), (), s32[]{:S(2)}) async-start(), calls=%async_computation.2 | async-start | bytes 36225024 | tf_op jit(solution)/shard_map/all_gather | solution.py:93
  7.9 567.1 %all-gather.7.cloned.1.call-start = ((), (), s32[]{:S(2)}) async-start(), calls=%async_computation.3 | async-start | bytes 17301504 | tf_op jit(solution)/shard_map/all_gather | solution.py:94
  8.7 1185.4 %all-reduce.33.cloned.1.call-start = ((), (), s32[]{:S(2)}) async-start(), calls=%async_computation.6 | async-start | bytes 139264
  33.3 217.7 %copy-start.58 = (f32[64]{0:T(128)}, f32[64]{0:T(128)S(1)}, u32[]{:S(2)}) copy-start(f32[64]{0:T(128)S(1)} %get-tuple-element.782) | copy-start | bytes 772
  33.3 217.7 %copy-start.60 = (f32[64]{0:T(128)}, f32[64]{0:T(128)S(1)}, u32[]{:S(2)}) copy-start(f32[64]{0:T(128)S(1)} %exp.80) | copy-start | bytes 772
  81.0 161.9 %copy-start.49 = (f32[2048]{0:T(1024)}, f32[2048]{0:T(1024)S(1)}, u32[]{:S(2)}) copy-start(f32[2048]{0:T(1024)S(1)} %convert_element_type.107) | copy-start | bytes 24580
  164.5 89.0 %copy-start.38 = (f32[4352]{0:T(1024)}, f32[4352]{0:T(1024)S(1)}, u32[]{:S(2)}) copy-start(f32[4352]{0:T(1024)S(1)} %get-tuple-element.724) | copy-start | bytes 52228
  164.5 89.0 %copy-start.40 = (f32[4352]{0:T(1024)}, f32[4352]{0:T(1024)S(1)}, u32[]{:S(2)}) copy-start(f32[4352]{0:T(1024)S(1)} %get-tuple-element.725) | copy-start | bytes 52228
  164.5 89.0 %copy-start.42 = (f32[4352]{0:T(1024)}, f32[4352]{0:T(1024)S(1)}, u32[]{:S(2)}) copy-start(f32[4352]{0:T(1024)S(1)} %get-tuple-element.726) | copy-start | bytes 52228
  164.5 89.0 %copy-start.44 = (f32[4352]{0:T(1024)}, f32[4352]{0:T(1024)S(1)}, u32[]{:S(2)}) copy-start(f32[4352]{0:T(1024)S(1)} %get-tuple-element.727) | copy-start | bytes 52228
  166.6 76.3 %copy-start.51 = (f32[512]{0:T(512)}, f32[512]{0:T(512)S(1)}, u32[]{:S(2)}) copy-start(f32[512]{0:T(512)S(1)} %fusion.91) | copy-start | bytes 6148
  166.6 76.3 %copy-start.56 = (f32[512]{0:T(512)}, f32[512]{0:T(512)S(1)}, u32[]{:S(2)}) copy-start(f32[512]{0:T(512)S(1)} %fusion.106) | copy-start | bytes 6148
  348.2 83.3 %copy-start.8 = (f32[64,128,64]{1,2,0:T(8,128)S(1)}, f32[64,128,64]{1,2,0:T(8,128)}, u32[]{:S(2)}) copy-start(f32[64,128,64]{1,2,0:T(8,128)} %bitcast_add_fusion.13) | copy-start | bytes 6291460 | tf_op jit(solution)/shard_map/jvp()/while
  348.2 83.3 %copy-start.18 = (pred[256,256]{1,0:T(8,128)(4,1)S(1)}, pred[256,256]{1,0:T(8,128)(4,1)}, u32[]{:S(2)}) copy-start(pred[256,256]{1,0:T(8,128)(4,1)} %copy-done.17) | copy-start | bytes 196612 | tf_op jit(solution)/shard_map/jvp()/while
  476.4 83.3 %copy-start.8 = (f32[64,128,64]{1,2,0:T(8,128)S(1)}, f32[64,128,64]{1,2,0:T(8,128)}, u32[]{:S(2)}) copy-start(f32[64,128,64]{1,2,0:T(8,128)} %bitcast_add_fusion.13) | copy-start | bytes 6291460 | tf_op jit(solution)/shard_map/jvp()/while
  476.4 83.3 %copy-start.18 = (pred[256,256]{1,0:T(8,128)(4,1)S(1)}, pred[256,256]{1,0:T(8,128)(4,1)}, u32[]{:S(2)}) copy-start(pred[256,256]{1,0:T(8,128)(4,1)} %copy-done.17) | copy-start | bytes 196612 | tf_op jit(solution)/shard_map/jvp()/while
  712.7 87.5 %copy-start.29 = (f32[2,256,128]{2,1,0:T(8,128)}, f32[2,256,128]{2,1,0:T(8,128)S(1)}, u32[]{:S(2)}) copy-start(f32[2,256,128]{2,1,0:T(8,128)S(1)} %fusion.209) | copy-start | bytes 786436 | tf_op jit(solution)/shard_map/transpose(jvp())/while
  712.9 87.3 %copy-start.27 = (f32[2,256,128]{2,1,0:T(8,128)}, f32[2,256,128]{2,1,0:T(8,128)S(1)}, u32[]{:S(2)}) copy-start(f32[2,256,128]{2,1,0:T(8,128)S(1)} %fusion.211) | copy-start | bytes 786436 | tf_op jit(solution)/shard_map/transpose(jvp())/while
  716.7 83.4 %copy-start.34 = (f32[2,256,64]{1,0,2:T(2,128)}, f32[2,256,64]{1,0,2:T(2,128)S(1)}, u32[]{:S(2)}) copy-start(f32[2,256,64]{1,0,2:T(2,128)S(1)} %dynamic_update_slice.85) | copy-start | bytes 393220 | tf_op jit(solution)/shard_map/transpose(jvp())/while
  716.9 83.3 %copy-start.31 = (f32[2,256,64]{2,1,0:T(8,128)}, f32[2,256,64]{2,1,0:T(8,128)S(1)}, u32[]{:S(2)}) copy-start(f32[2,256,64]{2,1,0:T(8,128)S(1)} %bitcast_dynamic-update-slice_fusion.4) | copy-start | bytes 393220 | tf_op jit(solution)/shard_map/transpose(jvp())/while
  800.2 29.1 %copy-start.23 = (pred[256,256]{1,0:T(8,128)(4,1)}, pred[256,256]{1,0:T(8,128)(4,1)S(1)}, u32[]{:S(2)}) copy-start(pred[256,256]{1,0:T(8,128)(4,1)S(1)} %iota_compare_fusion.4) | copy-start | bytes 196612 | tf_op jit(solution)/shard_map/transpose(jvp())/while
  885.0 87.5 %copy-start.29 = (f32[2,256,128]{2,1,0:T(8,128)}, f32[2,256,128]{2,1,0:T(8,128)S(1)}, u32[]{:S(2)}) copy-start(f32[2,256,128]{2,1,0:T(8,128)S(1)} %fusion.209) | copy-start | bytes 786436 | tf_op jit(solution)/shard_map/transpose(jvp())/while
  885.2 87.3 %copy-start.27 = (f32[2,256,128]{2,1,0:T(8,128)}, f32[2,256,128]{2,1,0:T(8,128)S(1)}, u32[]{:S(2)}) copy-start(f32[2,256,128]{2,1,0:T(8,128)S(1)} %fusion.211) | copy-start | bytes 786436 | tf_op jit(solution)/shard_map/transpose(jvp())/while
  889.1 83.4 %copy-start.34 = (f32[2,256,64]{1,0,2:T(2,128)}, f32[2,256,64]{1,0,2:T(2,128)S(1)}, u32[]{:S(2)}) copy-start(f32[2,256,64]{1,0,2:T(2,128)S(1)} %dynamic_update_slice.85) | copy-start | bytes 393220 | tf_op jit(solution)/shard_map/transpose(jvp())/while
  889.2 83.3 %copy-start.31 = (f32[2,256,64]{2,1,0:T(8,128)}, f32[2,256,64]{2,1,0:T(8,128)S(1)}, u32[]{:S(2)}) copy-start(f32[2,256,64]{2,1,0:T(8,128)S(1)} %bitcast_dynamic-update-slice_fusion.4) | copy-start | bytes 393220 | tf_op jit(solution)/shard_map/transpose(jvp())/while
  985.3 28.7 %copy-start.48 = (f32[32,1,128]{2,1,0:T(1,128)S(1)}, f32[32,1,128]{2,1,0:T(1,128)}, u32[]{:S(2)}) copy-start(f32[32,1,128]{2,1,0:T(1,128)} %convert_element_type.131) | copy-start | bytes 49156
  985.3 28.7 %copy-start.55 = (f32[512]{0:T(512)S(1)}, f32[512]{0:T(512)}, u32[]{:S(2)}) copy-start(f32[512]{0:T(512)} %copy-done.54) | copy-start | bytes 6148
  985.3 28.7 %copy-start.63 = (f32[512]{0:T(512)S(1)}, f32[512]{0:T(512)}, u32[]{:S(2)}) copy-start(f32[512]{0:T(512)} %fusion.105) | copy-start | bytes 6148
  1013.9 306.7 %reduce-scatter.6.cloned.1.call-start = ((), (), s32[]{:S(2)}) async-start(), calls=%async_computation.5 | async-start | bytes 17301504 | tf_op jit(solution)/shard_map/reduce_scatter | solution.py:134
  1030.4 668.0 %reduce-scatter.4.cloned.1.call-start = ((), (), s32[]{:S(2)}) async-start(), calls=%async_computation.4 | async-start | bytes 36225024 | tf_op jit(solution)/shard_map/reduce_scatter | solution.py:125
  1089.1 36.0 %copy-start.53 = (f32[4096]{0:T(1024)S(1)}, f32[4096]{0:T(1024)}, u32[]{:S(2)}) copy-start(f32[4096]{0:T(1024)} %get-tuple-element.718) | copy-start | bytes 49156
  1089.2 83.1 %copy-start.52 = (f32[512]{0:T(512)S(1)}, f32[512]{0:T(512)}, u32[]{:S(2)}) copy-start(f32[512]{0:T(512)} %copy-done.51) | copy-start | bytes 6148
  (67 other events, 725.2 us)
Sparse Core Ops, SparseCore 0:
  10.8 205.7 all-gather.4
  219.5 112.4 all-gather.6
  1014.0 119.0 all-reduce.32
  1135.3 185.2 reduce-scatter.5
  1322.7 375.5 reduce-scatter.3
where the time goes:
time: 1740 us; the launch traced here: 1710 us
  waiting for transfers between devices  552 us (32%)
  local copies, waits for them, and re-layouts  530 us (30%)
  matrix products  256 us (15%)
  blocking collectives  190 us (11%)
  other arithmetic  162 us (9%)
    dynamic_update_slice x12, local copies, waits for them, and re-layouts, ssd_mixer(): lax.scan(jax.checkpoint(partial(block_step, rounding=rounding)), zero_sta...  412 us
    reduce_scatter x1, waiting for transfers between devices, settle_grads(): lax.psum_scatter(lax.dot_general(columns, proj_grad, (((0,), (0,)), ((),...  376 us
    reduce_scatter x1, waiting for transfers between devices, settle_grads(): lax.psum_scatter(lax.dot_general(columns, branch_grad, (((0,), (0,)), (()...  125 us
    unnamed x3, blocking collectives  109 us
    dot_general x6, matrix products, block_step(): jnp.einsum('hts,shp->thp', mixing, x_heads, preferred_element_type=jnp.fl...  71.9 us
    all_gather x1, waiting for transfers between devices, fetch_weights(): lax.all_gather(in_part, ('wide', 'narrow'), axis=0, tiled=True)  50 us
    all_gather x1, blocking collectives, fetch_weights(): lax.all_gather(gain_part, ('wide', 'narrow'), axis=0, tiled=True)  42.1 us
    all_gather x1, blocking collectives, fetch_weights(): lax.all_gather(conv_part, ('wide', 'narrow'), axis=0, tiled=True)  39 us
  transfers between devices with their start and end apart: 5, of which 3 were waited for; matrix products, arithmetic and copies ran while one was open for 29% of the time, Pallas kernels for 0%

commit v1 on v0

--- a/solution.py
+++ b/solution.py
@@ -10,6 +10,28 @@
 KCONV = 4
 SPAN = 256
 EPS = 1e-05
+
+
+def laid_out(blocks, dim):
+    blocks = jnp.moveaxis(blocks, 0, dim)
+    shape = blocks.shape
+    return blocks.reshape(*shape[:dim], shape[dim] * shape[dim + 1], *shape[dim + 2 :])
+
+
+def collected_by_bits(x, axis):
+    size = lax.axis_size(axis)
+    blocks = x[None]
+    for level in range(size.bit_length() - 1):
+        bit = 1 << level
+        other = lax.ppermute(blocks, axis, [(i, i ^ bit) for i in range(size)])
+        both = jnp.stack([blocks, other])
+        upper = lax.axis_index(axis) >> level & 1
+        blocks = jnp.where(upper == 0, both, both[::-1]).reshape(-1, *x.shape)
+    return blocks
+
+
+def doubled_up(value, axis, dim):
+    return laid_out(collected_by_bits(value, axis), dim)
 
 
 def rounded(values):
@@ -90,7 +112,7 @@
 
 def fetch_weights(in_part, out_part, norm_part, conv_part, bias_part, gain_part):
     return (
-        lax.all_gather(in_part, ("wide", "narrow"), axis=0, tiled=True),
+        doubled_up(in_part, ("wide", "narrow"), 0),
         lax.all_gather(out_part, ("wide", "narrow"), axis=0, tiled=True),
         lax.all_gather(norm_part, ("wide", "narrow"), axis=0, tiled=True),
         lax.all_gather(conv_part, ("wide", "narrow"), axis=0, tiled=True),

time: 1740 us -> 2940 us (1.69)
  blocking collectives: 190 us -> 1000 us
  waiting for transfers between devices: 552 us -> 833 us
  other arithmetic: 162 us -> 266 us
    unnamed x3, blocking collectives: 109 us -> 925 us
    ppermute x0 -> x5, waiting for transfers between devices: none -> 334 us  [collected_by_bits(): other = lax.ppermute(blocks, axis, [(i, i ^ bit) for i in range(size)])]
    select_n x0 -> x4, other arithmetic: none -> 57.6 us  [collected_by_bits(): blocks = jnp.where(upper == 0, both, both[::-1]).reshape(-1, *x.shape)]
    all_gather x1 -> x0, waiting for transfers between devices: 50 us -> none  [fetch_weights(): lax.all_gather(in_part, ('wide', 'narrow'), axis=0, tiled=True)]
    another operation x16 -> x22, other arithmetic: 8.01 us -> 54 us  [the longest x6 46 us: collected_by_bits(): both = jnp.stack([blocks, other])]
  transfers between devices with their start and end apart: 5 -> 9, of which waited for: 3 -> 6; matrix products, arithmetic and copies ran while one was open for 29% -> 19% of each run, Pallas kernels for 0% -> 0%
where the time goes in v1:
time: 2940 us; the launch traced here: 2910 us
  blocking collectives  1000 us (34%)
  waiting for transfers between devices  833 us (28%)
  local copies, waits for them, and re-layouts  524 us (18%)
  other arithmetic  266 us (9%)
  matrix products  256 us (9%)
    unnamed x3, blocking collectives  925 us
    dynamic_update_slice x12, local copies, waits for them, and re-layouts, ssd_mixer(): lax.scan(jax.checkpoint(partial(block_step, rounding=rounding)), zero_sta...  412 us
    reduce_scatter x1, waiting for transfers between devices, settle_grads(): lax.psum_scatter(lax.dot_general(columns, proj_grad, (((0,), (0,)), ((),...  375 us
    ppermute x5, waiting for transfers between devices, collected_by_bits(): other = lax.ppermute(blocks, axis, [(i, i ^ bit) for i in range(size)])  334 us
    reduce_scatter x1, waiting for transfers between devices, settle_grads(): lax.psum_scatter(lax.dot_general(columns, branch_grad, (((0,), (0,)), (()...  124 us
    dot_general x6, matrix products, block_step(): jnp.einsum('hts,shp->thp', mixing, x_heads, preferred_element_type=jnp.fl...  71.9 us
  transfers between devices with their start and end apart: 9, of which 6 were waited for; matrix products, arithmetic and copies ran while one was open for 19% of the time, Pallas kernels for 0%

profile of v1, /device:TPU:1, one launch (start us, length us, event | category | flops | bytes accessed | tf_op | source)
XLA Modules:
  0.0 2906.3 jit_solution(6692500024197582943)
XLA Ops:
  15.8 48.1 %collective-permute-done.1 = bf16[2,64,8512]{2,1,0:T(8,128)(2,1)} collective-permute-done((bf16[2,64,8512]{2,1,0:T(8,128)(2,1)}, bf16[2,64,8512]{2,1,0:T(8,128)(2,1)}, u32[]{:S(2)}, u32[]{:S(2)}) %collective-permute-start.1) | collective-permute-done | bytes 2179104 | tf_op jit(solution)/shard_map/ppermute | solution.py:26
  69.9 94.6 %collective-permute-done.2 = bf16[4,64,8512]{2,1,0:T(8,128)(2,1)} collective-permute-done((bf16[4,64,8512]{2,1,0:T(8,128)(2,1)}, bf16[4,64,8512]{2,1,0:T(8,128)(2,1)}, u32[]{:S(2)}, u32[]{:S(2)}) %collective-permute-start.2) | collective-permute-done | bytes 4358176 | tf_op jit(solution)/shard_map/ppermute | solution.py:26
  184.6 188.0 %collective-permute-done.3 = bf16[8,64,8512]{2,1,0:T(8,128)(2,1)} collective-permute-done((bf16[8,64,8512]{2,1,0:T(8,128)(2,1)}, bf16[8,64,8512]{2,1,0:T(8,128)(2,1)}, u32[]{:S(2)}, u32[]{:S(2)}) %collective-permute-start.3) | collective-permute-done | bytes 8716320 | tf_op jit(solution)/shard_map/ppermute | solution.py:26
  393.7 389.2 %all-reduce.29 = (f32[64]{0:T(128)S(1)}, f32[64]{0:T(128)S(1)}, f32[64]{0:T(128)S(1)}) all-reduce(f32[64]{0:T(128)S(1)} %dynamic-update-slice.1, f32[64]{0:T(128)S(1)} %dynamic-update-slice.2, f32[64]{0:T(128)S(1)} %dynamic-update-slice.4), channel_id=1, replica_groups=mesh['wide'=8,'narrow'=4] {'wide'}, use_global_device_ids=true, to_apply=%add.17 | all-reduce | flops 192 | bytes 1536
  783.9 490.7 %all-reduce.30 = (bf16[2048]{0:T(1024)(128)(2,1)S(1)}, bf16[4352]{0:T(1024)(128)(2,1)S(1)}) all-reduce(bf16[2048]{0:T(1024)(128)(2,1)S(1)} %dynamic-update-slice, bf16[4352]{0:T(1024)(128)(2,1)S(1)} %dynamic-update-slice.3), channel_id=1, replica_groups=mesh['wide'=8,'narrow'=4] {'wide','narrow'}, use_global_device_ids=true, to_apply=%add.16 | all-reduce | flops 6400 | bytes 25600
  1274.6 41.6 %all-gather.1 = bf16[32,1,128]{2,1,0:T(2,128)(2,1)S(1)} all-gather(bf16[1,1,128]{2,1,0:T(2,128)(2,1)S(1)} %bitcast.452), channel_id=1, replica_groups=mesh['wide'=8,'narrow'=4] {'wide','narrow'}, dimensions={0}, use_global_device_ids=true | all-gather | bytes 8448 | tf_op jit(solution)/shard_map/all_gather | solution.py:120
  1317.6 37.0 %all-gather = bf16[32,136,4]{1,2,0:T(4,128)(2,1)S(1)} all-gather(bf16[1,136,4]{1,2,0:T(4,128)(2,1)S(1)} %bitcast.451), channel_id=1, replica_groups=mesh['wide'=8,'narrow'=4] {'wide','narrow'}, dimensions={0}, use_global_device_ids=true | all-gather | bytes 35904 | tf_op jit(solution)/shard_map/all_gather | solution.py:118
  1357.7 24.5 pad_maximum_fusion
  1382.2 35.3 %reverse_select_fusion = bf16[2,16,64,8512]{3,2,1,0:T(8,128)(2,1)} fusion(bf16[2,16,64,8512]{3,2,1,0:T(8,128)(2,1)} %pad_maximum_fusion, pred[]{:T(512)S(6)} %eq.28), kind=kLoop, calls=%fused_computation.124 | loop fusion | flops 17432576 | bytes 69730304 | tf_op jit(solution)/shard_map/jit(_where)/select_n | solution.py:29
  1417.5 26.0 fusion.102
  1454.0 23.8 fusion.81
  1501.5 257.0 %while.44 = (s32[]{:T(128)}, f32[64,128,64]{1,2,0:T(8,128)S(1)}, f32[2,256,4096]{1,0,2:T(2,128)}, f32[2,64,128,64]{2,3,1,0:T(8,128)}, f32[2,256,64]{1,2,0:T(8,12...) while((s32[]{:T(128)}, f32[64,128,64]{1,2,0:T(8,128)S(1)}, ...), condition=%wide.region_4.5_spmd.clone.clone, body=%wide.region_1.4_spmd.clone.clone.sunk | while | flops 1156104448 | bytes 122035080 | solution.py:97
  1527.7 19.2 copy.361
  1546.8 83.3 %dynamic_update_slice.87 = f32[2,256,4096]{1,0,2:T(2,128)} dynamic-update-slice(f32[2,256,4096]{1,0,2:T(2,128)} %get-tuple-element.1049, f32[1,256,4096]{1,0,2:T(1,128)} %copy.361, s32[]{:T(128)S(6)} %copy.378, s32[]{:T(128)} %constant.131.clone.1..sunk.1, s32[]{:T(128)} %constant.131.clone.1..sunk.1) | dynamic-update-slice | bytes 8388612 | tf_op jit(solution)/shard_map/jvp()/while/body/jit(dynamic_update_index_in_dim)/dynamic_update_slice | solution.py:97
  1655.9 19.2 copy.361
  1675.1 83.3 %dynamic_update_slice.87 = f32[2,256,4096]{1,0,2:T(2,128)} dynamic-update-slice(f32[2,256,4096]{1,0,2:T(2,128)} %get-tuple-element.1049, f32[1,256,4096]{1,0,2:T(1,128)} %copy.361, s32[]{:T(128)S(6)} %copy.378, s32[]{:T(128)} %constant.131.clone.1..sunk.1, s32[]{:T(128)} %constant.131.clone.1..sunk.1) | dynamic-update-slice | bytes 8388612 | tf_op jit(solution)/shard_map/jvp()/while/body/jit(dynamic_update_index_in_dim)/dynamic_update_slice | solution.py:97
  1773.7 17.8 multiply_reduce_fusion.10
  1791.5 18.1 multiply_reduce_fusion.9
  1828.4 342.9 %while.43 = (s32[]{:T(128)}, f32[64,128,64]{1,2,0:T(8,128)}, f32[2,256,4096]{1,0,2:T(2,128)}, f32[2,256,128]{2,1,0:T(8,128)}, f32[2,256,128]{2,1,0:T(8,128)}, /*...) while((s32[]{:T(128)}, f32[64,128,64]{1,2,0:T(8,128)}, ...), condition=%wide.region_19.20_spmd.clone, body=%wide.region_7.19_spmd.clone.sunk | while | flops 2587640576 | bytes 238366704 | solution.py:97
  1855.7 16.5 fusion.207
  1892.0 19.1 copy.353
  1915.6 83.3 %dynamic_update_slice.84 = f32[2,256,4096]{1,0,2:T(2,128)} dynamic-update-slice(f32[2,256,4096]{1,0,2:T(2,128)} %get-tuple-element.1092, f32[1,256,4096]{1,0,2:T(1,128)} %copy.353, s32[]{:T(128)S(6)} %sub.332, s32[]{:T(128)} %constant.131.clone.1..sunk, s32[]{:T(128)} %constant.131.clone.1..sunk) | dynamic-update-slice | bytes 8388612 | tf_op jit(solution)/shard_map/transpose(jvp())/while/body/jit(dynamic_update_index_in_dim)/dynamic_update_slice | solution.py:97
  2028.0 16.5 fusion.207
  2064.3 19.1 copy.353
  2087.9 83.3 %dynamic_update_slice.84 = f32[2,256,4096]{1,0,2:T(2,128)} dynamic-update-slice(f32[2,256,4096]{1,0,2:T(2,128)} %get-tuple-element.1092, f32[1,256,4096]{1,0,2:T(1,128)} %copy.353, s32[]{:T(128)S(6)} %sub.332, s32[]{:T(128)} %constant.131.clone.1..sunk, s32[]{:T(128)} %constant.131.clone.1..sunk) | dynamic-update-slice | bytes 8388612 | tf_op jit(solution)/shard_map/transpose(jvp())/while/body/jit(dynamic_update_index_in_dim)/dynamic_update_slice | solution.py:97
  2183.9 27.8 multiply_reduce_fusion.7
  2212.7 16.3 convolution_convert_fusion.1
  2258.1 28.2 convolution_convert_fusion
  2287.8 36.0 %fusion.88 = (f32[2048]{0:T(1024)S(1)}, f32[512]{0:T(512)S(1)}, f32[512,2048]{1,0:T(8,128)}) fusion(bf16[512,2048]{1,0:T(8,128)(2,1)S(1)} %copy-done.13, f32[512]{0:T(512)S(1)} %copy-done.57, f32[2048]{0:T(1024)S(1)} %copy-done.50, bf16[2048,8512]{1,0:T(8,128)(2,1)} %bitcast.431, f32[512,4096]{0,1:T(8,128)} %get-tuple-element.814, ...), kind=kOutput, calls=%fused_computation.182 | convolution fusion | flops 17871370240 | bytes 58609664 | tf_op jit(solution)/shard_map/dot_general | solution.py:229
  2323.8 44.6 %all-reduce.28 = (f32[2048]{0:T(1024)S(1)}, f32[4352]{0:T(1024)S(1)}, f32[4096]{0:T(1024)S(1)}, f32[256]{0:T(256)S(1)}, f32[256]{0:T(256)S(1)}, /*index=5*/f32[256]{0:T(256)S(1)}) all-reduce(f32[2048]{0:T(1024)S(1)} %get-tuple-element.722, ...), channel_id=4, replica_groups=mesh['wide'=8,'narrow'=4] {'wide','narrow'}, use_global_device_ids=true, to_apply=%region_24.25.clone | all-reduce | flops 11264 | bytes 90112
  2395.2 124.2 %reduce-scatter.6.cloned.1.call-done = bf16[128,2048]{1,0:T(8,128)(2,1)} async-done(((bf16[4096,2048]{1,0:T(8,128)(2,1)}), bf16[128,2048]{1,0:T(8,128)(2,1)}) %reduce-scatter.6.cloned.1.call-update) | async-done | bytes 524304 | tf_op jit(solution)/shard_map/reduce_scatter | solution.py:156
  2521.4 375.1 %reduce-scatter.4.cloned.1.call-done = bf16[64,8512]{1,0:T(8,128)(2,1)} async-done(((bf16[2048,8512]{1,0:T(8,128)(2,1)}), bf16[64,8512]{1,0:T(8,128)(2,1)}) %reduce-scatter.4.cloned.1.call-update) | async-done | bytes 1089552 | tf_op jit(solution)/shard_map/reduce_scatter | solution.py:147
  (446 shorter events, 358.2 us)
Async XLA Ops:
  7.2 1766.5 %all-gather.4.cloned.1.call-start = ((), (), s32[]{:S(2)}) async-start(), calls=%async_computation.2 | async-start | bytes 17301504 | tf_op jit(solution)/shard_map/all_gather | solution.py:116
  7.2 3.0 collective-permute-start
  13.4 50.4 %collective-permute-start.1 = (bf16[2,64,8512]{2,1,0:T(8,128)(2,1)}, bf16[2,64,8512]{2,1,0:T(8,128)(2,1)}, u32[]{:S(2)}, u32[]{:S(2)}) collective-permute-start(bf16[2,64,8512]{2,1,0:T(8,128)(2,1)} %get-tuple-element.824), channel_id=1, source_target_pairs={{0,2},{1,3},{2,0},{3,1},{4,6},{5,7},{6,4},{7,5},{8,10},{9,11},{10,... | collective-permute-start | bytes 6537224 | tf_op jit(solution)/shard_map/ppermute | solution.py:26
  68.7 95.7 %collective-permute-start.2 = (bf16[4,64,8512]{2,1,0:T(8,128)(2,1)}, bf16[4,64,8512]{2,1,0:T(8,128)(2,1)}, u32[]{:S(2)}, u32[]{:S(2)}) collective-permute-start(bf16[4,64,8512]{2,1,0:T(8,128)(2,1)} %bitcast.10), channel_id=1, source_target_pairs={{0,4},{1,5},{2,6},{3,7},{4,0},{5,1},{6,2},{7,3},{8,12},{9,13},{10,... | collective-permute-start | bytes 13074440 | tf_op jit(solution)/shard_map/ppermute | solution.py:26
  183.7 189.0 %collective-permute-start.3 = (bf16[8,64,8512]{2,1,0:T(8,128)(2,1)}, bf16[8,64,8512]{2,1,0:T(8,128)(2,1)}, u32[]{:S(2)}, u32[]{:S(2)}) collective-permute-start(bf16[8,64,8512]{2,1,0:T(8,128)(2,1)} %bitcast.428), channel_id=1, source_target_pairs={{0,8},{1,9},{2,10},{3,11},{4,12},{5,13},{6,14},{7,15},{8,0},{9,1},... | collective-permute-start | bytes 26148872 | tf_op jit(solution)/shard_map/ppermute | solution.py:26
  381.0 402.3 %copy-start.69 = (bf16[64]{0:T(256)(128)(2,1)S(1)}, bf16[64]{0:T(256)(128)(2,1)}, u32[]{:S(2)}) copy-start(bf16[64]{0:T(256)(128)(2,1)} %param.20) | copy-start | bytes 388
  381.1 402.6 %copy-start.70 = (bf16[136]{0:T(256)(128)(2,1)S(1)}, bf16[136]{0:T(256)(128)(2,1)}, u32[]{:S(2)}) copy-start(bf16[136]{0:T(256)(128)(2,1)} %param.22) | copy-start | bytes 820
  381.1 893.6 %copy-start.65 = (bf16[128]{0:T(256)(128)(2,1)S(1)}, bf16[128]{0:T(256)(128)(2,1)}, u32[]{:S(2)}) copy-start(bf16[128]{0:T(256)(128)(2,1)} %param.23) | copy-start | bytes 772
  381.1 936.5 %copy-start.62 = (bf16[136,4]{0,1:T(4,128)(2,1)S(1)}, bf16[136,4]{0,1:T(4,128)(2,1)}, u32[]{:S(2)}) copy-start(bf16[136,4]{0,1:T(4,128)(2,1)} %param.21) | copy-start | bytes 3268
  389.3 968.4 %collective-permute-start.4 = (bf16[16,64,8512]{2,1,0:T(8,128)(2,1)}, bf16[16,64,8512]{2,1,0:T(8,128)(2,1)}, u32[]{:S(2)}, u32[]{:S(2)}) collective-permute-start(bf16[16,64,8512]{2,1,0:T(8,128)(2,1)} %bitcast.16), channel_id=1, source_target_pairs={{0,16},{1,17},{2,18},{3,19},{4,20},{5,21},{6,22},{7,23},{8,24},{9,... | collective-permute-start | bytes 52297736 | tf_op jit(solution)/shard_map/ppermute | solution.py:26
  391.0 2002.8 %all-reduce.33.cloned.1.call-start = ((), (), s32[]{:S(2)}) async-start(), calls=%async_computation.5 | async-start | bytes 139264
  782.9 668.6 %copy-start.58 = (f32[64]{0:T(128)}, f32[64]{0:T(128)S(1)}, u32[]{:S(2)}) copy-start(f32[64]{0:T(128)S(1)} %get-tuple-element.782) | copy-start | bytes 772
  783.4 668.1 %copy-start.60 = (f32[64]{0:T(128)}, f32[64]{0:T(128)S(1)}, u32[]{:S(2)}) copy-start(f32[64]{0:T(128)S(1)} %exp.80) | copy-start | bytes 772
  1274.6 142.8 %copy-start.49 = (f32[2048]{0:T(1024)}, f32[2048]{0:T(1024)S(1)}, u32[]{:S(2)}) copy-start(f32[2048]{0:T(1024)S(1)} %convert_element_type.107) | copy-start | bytes 24580
  1355.5 98.5 %copy-start.38 = (f32[4352]{0:T(1024)}, f32[4352]{0:T(1024)S(1)}, u32[]{:S(2)}) copy-start(f32[4352]{0:T(1024)S(1)} %get-tuple-element.724) | copy-start | bytes 52228
  1355.5 98.5 %copy-start.40 = (f32[4352]{0:T(1024)}, f32[4352]{0:T(1024)S(1)}, u32[]{:S(2)}) copy-start(f32[4352]{0:T(1024)S(1)} %get-tuple-element.725) | copy-start | bytes 52228
  1355.6 98.5 %copy-start.42 = (f32[4352]{0:T(1024)}, f32[4352]{0:T(1024)S(1)}, u32[]{:S(2)}) copy-start(f32[4352]{0:T(1024)S(1)} %get-tuple-element.726) | copy-start | bytes 52228
  1355.6 98.5 %copy-start.44 = (f32[4352]{0:T(1024)}, f32[4352]{0:T(1024)S(1)}, u32[]{:S(2)}) copy-start(f32[4352]{0:T(1024)S(1)} %get-tuple-element.727) | copy-start | bytes 52228
  1546.8 83.3 %copy-start.8 = (f32[64,128,64]{1,2,0:T(8,128)S(1)}, f32[64,128,64]{1,2,0:T(8,128)}, u32[]{:S(2)}) copy-start(f32[64,128,64]{1,2,0:T(8,128)} %bitcast_add_fusion.13) | copy-start | bytes 6291460 | tf_op jit(solution)/shard_map/jvp()/while
  1546.8 83.3 %copy-start.18 = (pred[256,256]{1,0:T(8,128)(4,1)S(1)}, pred[256,256]{1,0:T(8,128)(4,1)}, u32[]{:S(2)}) copy-start(pred[256,256]{1,0:T(8,128)(4,1)} %copy-done.17) | copy-start | bytes 196612 | tf_op jit(solution)/shard_map/jvp()/while
  1675.1 83.3 %copy-start.8 = (f32[64,128,64]{1,2,0:T(8,128)S(1)}, f32[64,128,64]{1,2,0:T(8,128)}, u32[]{:S(2)}) copy-start(f32[64,128,64]{1,2,0:T(8,128)} %bitcast_add_fusion.13) | copy-start | bytes 6291460 | tf_op jit(solution)/shard_map/jvp()/while
  1675.1 83.3 %copy-start.18 = (pred[256,256]{1,0:T(8,128)(4,1)S(1)}, pred[256,256]{1,0:T(8,128)(4,1)}, u32[]{:S(2)}) copy-start(pred[256,256]{1,0:T(8,128)(4,1)} %copy-done.17) | copy-start | bytes 196612 | tf_op jit(solution)/shard_map/jvp()/while
  1911.3 87.5 %copy-start.29 = (f32[2,256,128]{2,1,0:T(8,128)}, f32[2,256,128]{2,1,0:T(8,128)S(1)}, u32[]{:S(2)}) copy-start(f32[2,256,128]{2,1,0:T(8,128)S(1)} %fusion.211) | copy-start | bytes 786436 | tf_op jit(solution)/shard_map/transpose(jvp())/while
  1911.5 87.3 %copy-start.27 = (f32[2,256,128]{2,1,0:T(8,128)}, f32[2,256,128]{2,1,0:T(8,128)S(1)}, u32[]{:S(2)}) copy-start(f32[2,256,128]{2,1,0:T(8,128)S(1)} %fusion.213) | copy-start | bytes 786436 | tf_op jit(solution)/shard_map/transpose(jvp())/while
  1915.4 83.4 %copy-start.34 = (f32[2,256,64]{1,0,2:T(2,128)}, f32[2,256,64]{1,0,2:T(2,128)S(1)}, u32[]{:S(2)}) copy-start(f32[2,256,64]{1,0,2:T(2,128)S(1)} %dynamic_update_slice.85) | copy-start | bytes 393220 | tf_op jit(solution)/shard_map/transpose(jvp())/while
  1915.5 83.3 %copy-start.31 = (f32[2,256,64]{2,1,0:T(8,128)}, f32[2,256,64]{2,1,0:T(8,128)S(1)}, u32[]{:S(2)}) copy-start(f32[2,256,64]{2,1,0:T(8,128)S(1)} %bitcast_dynamic-update-slice_fusion.4) | copy-start | bytes 393220 | tf_op jit(solution)/shard_map/transpose(jvp())/while
  2083.6 87.5 %copy-start.29 = (f32[2,256,128]{2,1,0:T(8,128)}, f32[2,256,128]{2,1,0:T(8,128)S(1)}, u32[]{:S(2)}) copy-start(f32[2,256,128]{2,1,0:T(8,128)S(1)} %fusion.211) | copy-start | bytes 786436 | tf_op jit(solution)/shard_map/transpose(jvp())/while
  2083.8 87.3 %copy-start.27 = (f32[2,256,128]{2,1,0:T(8,128)}, f32[2,256,128]{2,1,0:T(8,128)S(1)}, u32[]{:S(2)}) copy-start(f32[2,256,128]{2,1,0:T(8,128)S(1)} %fusion.213) | copy-start | bytes 786436 | tf_op jit(solution)/shard_map/transpose(jvp())/while
  2087.7 83.4 %copy-start.34 = (f32[2,256,64]{1,0,2:T(2,128)}, f32[2,256,64]{1,0,2:T(2,128)S(1)}, u32[]{:S(2)}) copy-start(f32[2,256,64]{1,0,2:T(2,128)S(1)} %dynamic_update_slice.85) | copy-start | bytes 393220 | tf_op jit(solution)/shard_map/transpose(jvp())/while
  2212.6 306.8 %reduce-scatter.6.cloned.1.call-start = ((), (), s32[]{:S(2)}) async-start(), calls=%async_computation.4 | async-start | bytes 17301504 | tf_op jit(solution)/shard_map/reduce_scatter | solution.py:156
  2229.1 667.4 %reduce-scatter.4.cloned.1.call-start = ((), (), s32[]{:S(2)}) async-start(), calls=%async_computation.3 | async-start | bytes 36225024 | tf_op jit(solution)/shard_map/reduce_scatter | solution.py:147
  2287.8 84.2 %copy-start.52 = (f32[512]{0:T(512)S(1)}, f32[512]{0:T(512)}, u32[]{:S(2)}) copy-start(f32[512]{0:T(512)} %copy-done.51) | copy-start | bytes 6148
  (79 other events, 1089.5 us)
Sparse Core Ops, SparseCore 0:
  391.1 517.2 all-gather.3
  2212.7 118.4 all-reduce.32
  2333.5 185.8 reduce-scatter.5
  2521.5 374.9 reduce-scatter.3
